TPU v7x, 256 devices: a whole 4x4x8 slice. The times are simulated.
256 devices in a mesh: ctx: 32 (over z, x_hi, core), tp: 8 (over y, x_lo).
Axes of the slice: x: 4 (x_hi: 2, x_lo: 2; x = x_hi * 2 + x_lo), y: 4, z: 8, core: 2. Of those that a mesh axis runs over, the one named last changes fastest.
Arguments:
- token_ids: int32 [4096], P('ctx'), may hold values from 0 to 511
- stream_table: bfloat16 [3, 512, 4096], P(None, None, 'tp'), may hold values from -6 to 6
- filters: float32 [256, 128], P('tp'), may hold values from -4 to 4
- proj_qk: bfloat16 [4096, 2, 4096], P(None, None, 'tp'), may hold values from -4 to 4
Outputs:
- attended: bfloat16 [4096, 4096], P('ctx', 'tp')
All inputs are finite; a program needn't handle non-finite values.
Results may differ from a plain program's by a relative error of at most 0.01.
Values may be sent and summed in bfloat16 or wider, within the bound.
No kernel may reach another device: no remote copies, remote signals or barrier semaphores. Data moves between devices by JAX's collectives and lax.ppermute only.
A program may use at most 64 MiB of HBM per device.

v0:
```python
import jax
import jax.numpy as jnp
from jax import lax
from jax.sharding import PartitionSpec as P

HEAD = 128
GROUP = 16
FLEN = 128
SPAN = 8


def from_behind(value, axis, steps):
    count = lax.axis_size(axis)
    leading, last = (max(0, -steps), min(count, count - steps))
    return lax.ppermute(value, axis, [(source, source + steps) for source in range(leading, last)])


def attend(state_now, queries, key_value, key_offset, query_offset, lowest):
    row_max, row_sum, numerator = state_now
    tok_rows = queries.shape[0]
    head_count = row_max.shape[0]
    span_rows = key_value.shape[1]
    query_heads = queries.reshape(tok_rows, head_count, HEAD)
    key_heads = key_value[0].reshape(span_rows, head_count, HEAD)
    value_heads = key_value[1].reshape(span_rows, head_count, HEAD)
    scores = jnp.einsum(
        "thd,shd->hts", query_heads, key_heads, preferred_element_type=jnp.float32
    ) * HEAD ** (-0.5)
    key_pos = key_offset + jnp.arange(span_rows, dtype=jnp.int32)
    query_pos = query_offset + jnp.arange(tok_rows, dtype=jnp.int32)
    allowed = (key_pos[None, :] >= lowest) & (key_pos[None, :] <= query_pos[:, None])
    masked = jnp.where(allowed[None], scores, -1e30)
    new_max = jnp.maximum(row_max, jnp.max(masked, axis=2))
    rescale = jnp.exp(row_max - new_max)
    weights = jnp.where(allowed[None], jnp.exp(masked - new_max[:, :, None]), 0.0)
    row_sum = row_sum * rescale + jnp.sum(weights, axis=2)
    partial_out = jnp.einsum(
        "hts,shd->thd",
        weights.astype(jnp.bfloat16),
        value_heads,
        preferred_element_type=jnp.float32,
    )
    numerator = numerator * jnp.transpose(rescale)[:, :, None] + partial_out
    return (new_max, row_sum, numerator)


def toeplitz_taps(filters):
    groups_here = filters.shape[0]
    padded_taps = jnp.concatenate(
        [
            jnp.zeros((groups_here, 1), jnp.float32),
            filters[:, ::-1],
            jnp.zeros((groups_here, FLEN), jnp.float32),
        ],
        axis=1,
    )
    tiled = jnp.tile(padded_taps, (1, FLEN))[:, : FLEN * 2 * FLEN]
    return tiled.reshape(groups_here, FLEN, 2 * FLEN)


def shards(token_ids, stream_table, filters, proj_qk):
    tok_rows = token_ids.shape[0]
    chan_width = stream_table.shape[2]
    onehot = (
        token_ids[:, None] == jnp.arange(stream_table.shape[1], dtype=jnp.int32)[None, :]
    ).astype(jnp.bfloat16)
    streams = jnp.einsum("tv,svc->stc", onehot, stream_table, preferred_element_type=jnp.float32)
    mixed_in = (streams[1] * streams[2]).astype(jnp.bfloat16)
    rim_rows = from_behind(mixed_in[tok_rows - (FLEN - 1) :], "ctx", 1)
    extended = jnp.concatenate(
        [jnp.zeros((1, chan_width), jnp.bfloat16), rim_rows, mixed_in], axis=0
    )
    block_count = tok_rows // FLEN
    stacked = extended.reshape(block_count + 1, FLEN, chan_width).astype(jnp.float32)
    paired = jnp.concatenate([stacked[:-1], stacked[1:]], axis=1)
    groups_here = filters.shape[0]
    paired = paired.reshape(block_count, 2 * FLEN, groups_here, GROUP)
    toeplitz = toeplitz_taps(filters)
    conv = jnp.einsum("gos,nsgc->nogc", toeplitz, paired, precision=lax.Precision.HIGHEST).reshape(
        tok_rows, chan_width
    )
    gated = (streams[0] * conv).astype(jnp.bfloat16)
    weights_local = proj_qk.reshape(proj_qk.shape[0], 2 * chan_width)
    projected = jnp.dot(
        lax.all_gather(gated, "tp", axis=1, tiled=True),
        weights_local,
        preferred_element_type=jnp.float32,
    )
    queries = projected[:, :chan_width].astype(jnp.bfloat16)
    keys = projected[:, chan_width:].astype(jnp.bfloat16)
    head_count = chan_width // HEAD
    position = lax.axis_index("ctx")
    query_offset = position * tok_rows
    lowest = jnp.maximum(position - SPAN + 1, 0) * tok_rows
    key_value = jnp.stack([keys, gated])
    initial = (
        jnp.full((head_count, tok_rows), -1e30, jnp.float32),
        jnp.zeros((head_count, tok_rows), jnp.float32),
        jnp.zeros((tok_rows, head_count, HEAD), jnp.float32),
    )
    state_now = attend(initial, queries, key_value, query_offset, query_offset, lowest)
    moving = key_value
    for distance in range(1, SPAN):
        moving = from_behind(moving, "ctx", 1)
        state_now = attend(
            state_now, queries, moving, query_offset - distance * tok_rows, query_offset, lowest
        )
    row_max, row_sum, numerator = state_now
    result = numerator / jnp.transpose(row_sum)[:, :, None]
    return result.reshape(tok_rows, chan_width).astype(jnp.bfloat16)


def solution(mesh):
    placed = (P("ctx"), P(None, None, "tp"), P("tp", None), P(None, None, "tp"))
    return jax.shard_map(
        shards, mesh=mesh, in_specs=placed, out_specs=P("ctx", "tp"), check_vma=False
    )
```

profile of v0, /device:TPU:128, one launch (start us, length us, event | category | flops | bytes accessed | tf_op | source)
XLA Modules:
  0.0 192.1 jit_solution(15303166851761119187)
XLA Ops:
  6.5 1.4 copy-done
  7.9 1.1 convolution_bitcast_fusion
  9.1 1.9 collective-permute-start
  11.0 0.8 rev.3
  12.0 3.1 %tile.4 = f32[32,128,257]{2,1,0:T(8,128)} broadcast(f32[32,257]{1,0:T(8,128)S(1)} %maximum_maximum_fusion), dimensions={0,2} | broadcast | bytes 4243584 | tf_op jit(solution)/shard_map/tile | solution.py:57
  15.0 6.7 %tile.10 = f32[32,32896]{1,0:T(8,128)} reshape(f32[32,128,257]{2,1,0:T(8,128)} %tile.4) | data formatting | bytes 8421376 | tf_op jit(solution)/shard_map/tile | solution.py:57
  21.7 2.2 %slice-done = f32[32,32768]{1,0:T(8,128)S(1)} async-done(((f32[32,32896]{1,0:T(8,128)}), f32[32,32768]{1,0:T(8,128)S(1)}, s32[]{:S(2)}) %slice-start) | async-done | bytes 4194328 | tf_op jit(solution)/shard_map/slice | solution.py:57
  23.9 3.2 %copy.95 = f32[4,8,128,256]{3,2,1,0:T(8,128)} copy(f32[4,8,128,256]{3,1,2,0:T(8,128)S(1)} %bitcast.264) | data formatting | bytes 8388608
  27.4 0.8 pad_maximum_fusion
  28.2 1.2 copy.41
  29.4 5.3 %fusion.141 = f32[32,16,128]{2,1,0:T(8,128)S(1)} fusion(f32[256,32,16]{0,2,1:T(8,128)S(1)} %bitcast.270, f32[32,128,256]{2,1,0:T(8,128)} %bitcast.265), kind=kOutput, calls=%fused_computation.218 | convolution fusion | flops 201326592 | bytes 4980736 | tf_op jit(solution)/shard_map/gos,nsgc->nogc/dot_general | solution.py:79
  35.6 9.4 %copy.96 = bf16[512,8,2,512]{3,1,2,0:T(8,128)(2,1)} copy(bf16[512,8,2,512]{3,2,1,0:T(2,128)(2,1)} %bitcast.266) | data formatting | bytes 16777216
  47.9 33.9 %all-gather.2.cloned.1.call-done = bf16[128,4096]{1,0:T(8,128)(2,1)} async-done(((bf16[128,512]{1,0:T(8,128)(2,1)}), bf16[128,4096]{1,0:T(8,128)(2,1)}) %all-gather.2.cloned.1.call-update) | async-done | bytes 1048592 | tf_op jit(solution)/shard_map/all_gather | solution.py:85
  81.8 5.0 %convolution_convert_fusion = bf16[128,1024]{1,0:T(8,128)(2,1)S(1)} fusion(bf16[128,4096]{1,0:T(8,128)(2,1)} %all-gather.2.cloned.1.call-done, bf16[4096,1024]{1,0:T(8,128)(2,1)} %bitcast.263), kind=kOutput, calls=%fused_computation.1 | convolution fusion | flops 1073872896 | bytes 9699328 | tf_op jit(solution)/shard_map/dot_general | solution.py:84
  86.9 1.9 collective-permute-start.1
  88.9 0.9 compare_and_fusion.5
  89.9 0.8 copy.85
  90.7 1.5 fusion.140
  92.2 6.0 %collective-permute-done.1 = bf16[2,128,512]{2,1,0:T(8,128)(2,1)S(1)} collective-permute-done((bf16[2,128,512]{2,1,0:T(8,128)(2,1)S(1)}, bf16[2,128,512]{2,1,0:T(8,128)(2,1)S(1)}, u32[]{:S(2)}, u32[]{:S(2)}) %collective-permute-start.1) | collective-permute-done | bytes 262176 | tf_op jit(solution)/shard_map/ppermute | solution.py:15
  98.2 1.9 collective-permute-start.2
  100.6 8.9 %collective-permute-done.2 = bf16[2,128,512]{2,1,0:T(8,128)(2,1)S(1)} collective-permute-done((bf16[2,128,512]{2,1,0:T(8,128)(2,1)S(1)}, bf16[2,128,512]{2,1,0:T(8,128)(2,1)S(1)}, u32[]{:S(2)}, u32[]{:S(2)}) %collective-permute-start.2) | collective-permute-done | bytes 262176 | tf_op jit(solution)/shard_map/ppermute | solution.py:15
  109.5 1.9 collective-permute-start.3
  112.5 8.3 %collective-permute-done.3 = bf16[2,128,512]{2,1,0:T(8,128)(2,1)S(1)} collective-permute-done((bf16[2,128,512]{2,1,0:T(8,128)(2,1)S(1)}, bf16[2,128,512]{2,1,0:T(8,128)(2,1)S(1)}, u32[]{:S(2)}, u32[]{:S(2)}) %collective-permute-start.3) | collective-permute-done | bytes 262176 | tf_op jit(solution)/shard_map/ppermute | solution.py:15
  120.8 1.9 collective-permute-start.4
  123.5 1.1 fusion.137
  124.7 7.4 %collective-permute-done.4 = bf16[2,128,512]{2,1,0:T(8,128)(2,1)S(1)} collective-permute-done((bf16[2,128,512]{2,1,0:T(8,128)(2,1)S(1)}, bf16[2,128,512]{2,1,0:T(8,128)(2,1)S(1)}, u32[]{:S(2)}, u32[]{:S(2)}) %collective-permute-start.4) | collective-permute-done | bytes 262176 | tf_op jit(solution)/shard_map/ppermute | solution.py:15
  132.8 1.9 collective-permute-start.5
  134.7 1.2 fusion.136
  137.3 6.9 %collective-permute-done.5 = bf16[2,128,512]{2,1,0:T(8,128)(2,1)} collective-permute-done((bf16[2,128,512]{2,1,0:T(8,128)(2,1)S(1)}, bf16[2,128,512]{2,1,0:T(8,128)(2,1)}, u32[]{:S(2)}, u32[]{:S(2)}) %collective-permute-start.5) | collective-permute-done | bytes 262176 | tf_op jit(solution)/shard_map/ppermute | solution.py:15
  144.2 2.1 %collective-permute-start.6 = (bf16[2,128,512]{2,1,0:T(8,128)(2,1)}, bf16[2,128,512]{2,1,0:T(8,128)(2,1)}, u32[]{:S(2)}, u32[]{:S(2)}) collective-permute-start(bf16[2,128,512]{2,1,0:T(8,128)(2,1)} %collective-permute-done.5), channel_id=1, source_target_pairs={{0,8},{8,16},{16,24},{24,32},{32,40},{40,48},{48,56},{56,64},{64,7... | collective-permute-start | bytes 786440 | tf_op jit(solution)/shard_map/ppermute | solution.py:15
  146.3 1.0 fusion.128
  148.1 1.7 fusion.135
  149.9 5.9 %collective-permute-done.6 = bf16[2,128,512]{2,1,0:T(8,128)(2,1)} collective-permute-done((bf16[2,128,512]{2,1,0:T(8,128)(2,1)}, bf16[2,128,512]{2,1,0:T(8,128)(2,1)}, u32[]{:S(2)}, u32[]{:S(2)}) %collective-permute-start.6) | collective-permute-done | bytes 262176 | tf_op jit(solution)/shard_map/ppermute | solution.py:15
  155.8 1.9 %collective-permute-start.7 = (bf16[2,128,512]{2,1,0:T(8,128)(2,1)}, bf16[2,128,512]{2,1,0:T(8,128)(2,1)}, u32[]{:S(2)}, u32[]{:S(2)}) collective-permute-start(bf16[2,128,512]{2,1,0:T(8,128)(2,1)} %collective-permute-done.6), channel_id=1, source_target_pairs={{0,8},{8,16},{16,24},{24,32},{32,40},{40,48},{48,56},{56,64},{64,7... | collective-permute-start | bytes 786440 | tf_op jit(solution)/shard_map/ppermute | solution.py:15
  157.8 1.0 fusion.127
  160.2 1.7 fusion.134
  161.9 5.5 %collective-permute-done.7 = bf16[2,128,512]{2,1,0:T(8,128)(2,1)} collective-permute-done((bf16[2,128,512]{2,1,0:T(8,128)(2,1)}, bf16[2,128,512]{2,1,0:T(8,128)(2,1)}, u32[]{:S(2)}, u32[]{:S(2)}) %collective-permute-start.7) | collective-permute-done | bytes 262176 | tf_op jit(solution)/shard_map/ppermute | solution.py:15
  167.4 1.7 fusion.126
  169.1 1.6 reshape_squeeze.54
  170.7 1.7 copy.92
  172.4 1.3 fusion.133
  174.4 0.8 fusion.43
  175.3 0.8 fusion.39
  176.9 0.8 fusion.35
  177.7 0.8 fusion.33
  179.3 1.0 fusion.29
  181.0 1.2 fusion.23
  182.3 0.9 fusion.21
  (122 shorter events, 16.0 us)
Async XLA Ops:
  6.5 1.4 copy-start
  6.5 75.2 %all-gather.2.cloned.1.call-start = ((), (), s32[]{:S(2)}) async-start(), calls=%async_computation | async-start | bytes 1179648 | tf_op jit(solution)/shard_map/all_gather | solution.py:85
  9.1 18.1 %collective-permute-start = (bf16[127,512]{1,0:T(8,128)(2,1)S(1)}, bf16[127,512]{1,0:T(8,128)(2,1)S(1)}, u32[]{:S(2)}, u32[]{:S(2)}) collective-permute-start(bf16[127,512]{1,0:T(8,128)(2,1)S(1)} %slice_bitcast_fusion.3), channel_id=1, source_target_pairs={{0,8},{8,16},{16,24},{24,32},{32,40},{40,48},{48,56},{56,64},{64,7... | collective-permute-start | bytes 390152 | tf_op jit(solution)/shard_map/ppermute | solution.py:15
  21.7 2.2 %slice-start = ((f32[32,32896]{1,0:T(8,128)}), f32[32,32768]{1,0:T(8,128)S(1)}, s32[]{:S(2)}) async-start(f32[32,32896]{1,0:T(8,128)} %tile.10), calls=%async_computation.1 | async-start | bytes 8388608 | tf_op jit(solution)/shard_map/slice | solution.py:57
  81.8 7.0 %copy-start.24 = (pred[128]{0:T(512)(128)(4,1)S(1)}, pred[128]{0:T(512)(128)(4,1)}, u32[]{:S(2)}) copy-start(pred[128]{0:T(512)(128)(4,1)} %get-tuple-element.76) | copy-start | bytes 388
  81.8 7.1 %copy-start.25 = (s32[128]{0:T(128)S(1)}, s32[128]{0:T(128)}, u32[]{:S(2)}) copy-start(s32[128]{0:T(128)} %get-tuple-element.81) | copy-start | bytes 1540
  81.8 7.1 %copy-start.26 = (s32[128]{0:T(128)S(1)}, s32[128]{0:T(128)}, u32[]{:S(2)}) copy-start(s32[128]{0:T(128)} %get-tuple-element.82) | copy-start | bytes 1540
  81.8 7.1 %copy-start.27 = (s32[128]{0:T(128)S(1)}, s32[128]{0:T(128)}, u32[]{:S(2)}) copy-start(s32[128]{0:T(128)} %get-tuple-element.79) | copy-start | bytes 1540
  81.8 7.1 %copy-start.28 = (s32[128]{0:T(128)S(1)}, s32[128]{0:T(128)}, u32[]{:S(2)}) copy-start(s32[128]{0:T(128)} %get-tuple-element.80) | copy-start | bytes 1540
  81.8 7.1 %copy-start.29 = (s32[128]{0:T(128)S(1)}, s32[128]{0:T(128)}, u32[]{:S(2)}) copy-start(s32[128]{0:T(128)} %get-tuple-element.77) | copy-start | bytes 1540
  81.8 7.1 %copy-start.30 = (s32[128]{0:T(128)S(1)}, s32[128]{0:T(128)}, u32[]{:S(2)}) copy-start(s32[128]{0:T(128)} %get-tuple-element.78) | copy-start | bytes 1540
  81.8 7.1 %copy-start.31 = (s32[128]{0:T(128)S(1)}, s32[128]{0:T(128)}, u32[]{:S(2)}) copy-start(s32[128]{0:T(128)} %get-tuple-element.83) | copy-start | bytes 1540
  86.8 25.6 %copy-start.16 = (bf16[16,4,8,128]{3,2,1,0:T(8,128)(2,1)}, bf16[16,4,8,128]{3,2,1,0:T(8,128)(2,1)S(1)}, u32[]{:S(2)}) copy-start(bf16[16,4,8,128]{3,2,1,0:T(8,128)(2,1)S(1)} %get-tuple-element.41) | copy-start | bytes 393220
  86.9 11.3 %collective-permute-start.1 = (bf16[2,128,512]{2,1,0:T(8,128)(2,1)S(1)}, bf16[2,128,512]{2,1,0:T(8,128)(2,1)S(1)}, u32[]{:S(2)}, u32[]{:S(2)}) collective-permute-start(bf16[2,128,512]{2,1,0:T(8,128)(2,1)S(1)} %pad_maximum_fusion.1), channel_id=1, source_target_pairs={{0,8},{8,16},{16,24},{24,32},{32,40},{40,48},{48,56},{56,64},{64,7... | collective-permute-start | bytes 786440 | tf_op jit(solution)/shard_map/ppermute | solution.py:15
  89.8 57.5 %copy-start.8 = (pred[128,128]{0,1:T(8,128)(4,1)}, pred[128,128]{0,1:T(8,128)(4,1)S(1)}, u32[]{:S(2)}) copy-start(pred[128,128]{0,1:T(8,128)(4,1)S(1)} %get-tuple-element.47) | copy-start | bytes 49156
  89.8 57.5 %copy-start.10 = (pred[128,128]{0,1:T(8,128)(4,1)}, pred[128,128]{0,1:T(8,128)(4,1)S(1)}, u32[]{:S(2)}) copy-start(pred[128,128]{0,1:T(8,128)(4,1)S(1)} %get-tuple-element.46) | copy-start | bytes 49156
  89.8 57.5 %copy-start.12 = (pred[128,128]{0,1:T(8,128)(4,1)}, pred[128,128]{0,1:T(8,128)(4,1)S(1)}, u32[]{:S(2)}) copy-start(pred[128,128]{0,1:T(8,128)(4,1)S(1)} %get-tuple-element.45) | copy-start | bytes 49156
  89.8 57.5 %copy-start.14 = (pred[128,128]{0,1:T(8,128)(4,1)}, pred[128,128]{0,1:T(8,128)(4,1)S(1)}, u32[]{:S(2)}) copy-start(pred[128,128]{0,1:T(8,128)(4,1)S(1)} %get-tuple-element.52) | copy-start | bytes 49156
  89.8 57.5 %copy-start.15 = (pred[128,128]{0,1:T(8,128)(4,1)}, pred[128,128]{0,1:T(8,128)(4,1)S(1)}, u32[]{:S(2)}) copy-start(pred[128,128]{0,1:T(8,128)(4,1)S(1)} %get-tuple-element.51) | copy-start | bytes 49156
  89.9 58.3 %copy-start.6 = (pred[128,128]{0,1:T(8,128)(4,1)}, pred[128,128]{0,1:T(8,128)(4,1)S(1)}, u32[]{:S(2)}) copy-start(pred[128,128]{0,1:T(8,128)(4,1)S(1)} %get-tuple-element.48) | copy-start | bytes 49156
  92.2 44.5 %copy-start.19 = (f32[4,128]{1,0:T(4,128)S(1)}, f32[4,128]{1,0:T(4,128)}, u32[]{:S(2)}) copy-start(f32[4,128]{1,0:T(4,128)} %get-tuple-element.67) | copy-start | bytes 6148
  98.2 11.3 %collective-permute-start.2 = (bf16[2,128,512]{2,1,0:T(8,128)(2,1)S(1)}, bf16[2,128,512]{2,1,0:T(8,128)(2,1)S(1)}, u32[]{:S(2)}, u32[]{:S(2)}) collective-permute-start(bf16[2,128,512]{2,1,0:T(8,128)(2,1)S(1)} %collective-permute-done.1), channel_id=1, source_target_pairs={{0,8},{8,16},{16,24},{24,32},{32,40},{40,48},{48,56},{56,64},{64,7... | collective-permute-start | bytes 786440 | tf_op jit(solution)/shard_map/ppermute | solution.py:15
  100.5 55.3 %copy-start.20 = (f32[4,128]{1,0:T(4,128)}, f32[4,128]{1,0:T(4,128)S(1)}, u32[]{:S(2)}) copy-start(f32[4,128]{1,0:T(4,128)S(1)} %get-tuple-element.65) | copy-start | bytes 6148
  109.5 11.3 %collective-permute-start.3 = (bf16[2,128,512]{2,1,0:T(8,128)(2,1)S(1)}, bf16[2,128,512]{2,1,0:T(8,128)(2,1)S(1)}, u32[]{:S(2)}, u32[]{:S(2)}) collective-permute-start(bf16[2,128,512]{2,1,0:T(8,128)(2,1)S(1)} %collective-permute-done.2), channel_id=1, source_target_pairs={{0,8},{8,16},{16,24},{24,32},{32,40},{40,48},{48,56},{56,64},{64,7... | collective-permute-start | bytes 786440 | tf_op jit(solution)/shard_map/ppermute | solution.py:15
  112.5 43.3 %copy-start.22 = (f32[4,128]{1,0:T(4,128)}, f32[4,128]{1,0:T(4,128)S(1)}, u32[]{:S(2)}) copy-start(f32[4,128]{1,0:T(4,128)S(1)} %get-tuple-element.63) | copy-start | bytes 6148
  120.8 11.3 %collective-permute-start.4 = (bf16[2,128,512]{2,1,0:T(8,128)(2,1)S(1)}, bf16[2,128,512]{2,1,0:T(8,128)(2,1)S(1)}, u32[]{:S(2)}, u32[]{:S(2)}) collective-permute-start(bf16[2,128,512]{2,1,0:T(8,128)(2,1)S(1)} %collective-permute-done.3), channel_id=1, source_target_pairs={{0,8},{8,16},{16,24},{24,32},{32,40},{40,48},{48,56},{56,64},{64,7... | collective-permute-start | bytes 786440 | tf_op jit(solution)/shard_map/ppermute | solution.py:15
  124.7 31.1 %copy-start.21 = (f32[4,128]{1,0:T(4,128)}, f32[4,128]{1,0:T(4,128)S(1)}, u32[]{:S(2)}) copy-start(f32[4,128]{1,0:T(4,128)S(1)} %get-tuple-element.61) | copy-start | bytes 6148
  132.8 11.4 %collective-permute-start.5 = (bf16[2,128,512]{2,1,0:T(8,128)(2,1)S(1)}, bf16[2,128,512]{2,1,0:T(8,128)(2,1)}, u32[]{:S(2)}, u32[]{:S(2)}) collective-permute-start(bf16[2,128,512]{2,1,0:T(8,128)(2,1)S(1)} %collective-permute-done.4), channel_id=1, source_target_pairs={{0,8},{8,16},{16,24},{24,32},{32,40},{40,48},{48,56},{56,64},{64,7... | collective-permute-start | bytes 786440 | tf_op jit(solution)/shard_map/ppermute | solution.py:15
  135.9 19.9 %copy-start.23 = (f32[4,128]{1,0:T(4,128)}, f32[4,128]{1,0:T(4,128)S(1)}, u32[]{:S(2)}) copy-start(f32[4,128]{1,0:T(4,128)S(1)} %get-tuple-element.59) | copy-start | bytes 6148
  144.2 11.6 %collective-permute-start.6 = (bf16[2,128,512]{2,1,0:T(8,128)(2,1)}, bf16[2,128,512]{2,1,0:T(8,128)(2,1)}, u32[]{:S(2)}, u32[]{:S(2)}) collective-permute-start(bf16[2,128,512]{2,1,0:T(8,128)(2,1)} %collective-permute-done.5), channel_id=1, source_target_pairs={{0,8},{8,16},{16,24},{24,32},{32,40},{40,48},{48,56},{56,64},{64,7... | collective-permute-start | bytes 786440 | tf_op jit(solution)/shard_map/ppermute | solution.py:15
  155.8 11.6 %collective-permute-start.7 = (bf16[2,128,512]{2,1,0:T(8,128)(2,1)}, bf16[2,128,512]{2,1,0:T(8,128)(2,1)}, u32[]{:S(2)}, u32[]{:S(2)}) collective-permute-start(bf16[2,128,512]{2,1,0:T(8,128)(2,1)} %collective-permute-done.6), channel_id=1, source_target_pairs={{0,8},{8,16},{16,24},{24,32},{32,40},{40,48},{48,56},{56,64},{64,7... | collective-permute-start | bytes 786440 | tf_op jit(solution)/shard_map/ppermute | solution.py:15
  172.4 10.8 %copy-start.1 = (bf16[1,128,512]{1,2,0:T(8,128)(2,1)S(1)}, bf16[1,128,512]{1,2,0:T(8,128)(2,1)}, u32[]{:S(2)}) copy-start(bf16[1,128,512]{1,2,0:T(8,128)(2,1)} %copy.87) | copy-start | bytes 393220
  172.4 10.8 %copy-start.13 = (pred[128,128]{0,1:T(8,128)(4,1)S(1)}, pred[128,128]{0,1:T(8,128)(4,1)}, u32[]{:S(2)}) copy-start(pred[128,128]{0,1:T(8,128)(4,1)} %copy-done.12) | copy-start | bytes 49156
  172.4 11.0 %copy-start.2 = (bf16[1,128,512]{1,2,0:T(8,128)(2,1)S(1)}, bf16[1,128,512]{1,2,0:T(8,128)(2,1)}, u32[]{:S(2)}) copy-start(bf16[1,128,512]{1,2,0:T(8,128)(2,1)} %copy.88) | copy-start | bytes 393220
  172.4 11.0 %copy-start.11 = (pred[128,128]{0,1:T(8,128)(4,1)S(1)}, pred[128,128]{0,1:T(8,128)(4,1)}, u32[]{:S(2)}) copy-start(pred[128,128]{0,1:T(8,128)(4,1)} %copy-done.10) | copy-start | bytes 49156
  172.4 11.2 %copy-start.3 = (bf16[1,128,512]{1,2,0:T(8,128)(2,1)S(1)}, bf16[1,128,512]{1,2,0:T(8,128)(2,1)}, u32[]{:S(2)}) copy-start(bf16[1,128,512]{1,2,0:T(8,128)(2,1)} %copy.89) | copy-start | bytes 393220
  172.4 11.2 %copy-start.9 = (pred[128,128]{0,1:T(8,128)(4,1)S(1)}, pred[128,128]{0,1:T(8,128)(4,1)}, u32[]{:S(2)}) copy-start(pred[128,128]{0,1:T(8,128)(4,1)} %copy-done.8) | copy-start | bytes 49156
  172.4 11.4 %copy-start.4 = (bf16[1,128,512]{1,2,0:T(8,128)(2,1)S(1)}, bf16[1,128,512]{1,2,0:T(8,128)(2,1)}, u32[]{:S(2)}) copy-start(bf16[1,128,512]{1,2,0:T(8,128)(2,1)} %copy.90) | copy-start | bytes 393220
  172.4 11.4 %copy-start.7 = (pred[128,128]{0,1:T(8,128)(4,1)S(1)}, pred[128,128]{0,1:T(8,128)(4,1)}, u32[]{:S(2)}) copy-start(pred[128,128]{0,1:T(8,128)(4,1)} %copy-done.6) | copy-start | bytes 49156
  173.7 10.4 %copy-start.5 = (bf16[1,128,512]{1,2,0:T(8,128)(2,1)S(1)}, bf16[1,128,512]{1,2,0:T(8,128)(2,1)}, u32[]{:S(2)}) copy-start(bf16[1,128,512]{1,2,0:T(8,128)(2,1)} %copy.91) | copy-start | bytes 393220
  175.3 9.0 %copy-start.17 = (bf16[1,128,512]{1,2,0:T(8,128)(2,1)S(1)}, bf16[1,128,512]{1,2,0:T(8,128)(2,1)}, u32[]{:S(2)}) copy-start(bf16[1,128,512]{1,2,0:T(8,128)(2,1)} %copy.92) | copy-start | bytes 393220
  175.3 9.0 %copy-start.18 = (pred[128,128]{0,1:T(8,128)(4,1)S(1)}, pred[128,128]{0,1:T(8,128)(4,1)}, u32[]{:S(2)}) copy-start(pred[128,128]{0,1:T(8,128)(4,1)} %get-tuple-element.50) | copy-start | bytes 49156
Sparse Core Ops, SparseCore 0:
  35.7 46.0 all-gather.1
where the time goes:
time: 193 us; the launch traced here: 192 us
  waiting for transfers between devices  82.9 us (43%)
  local copies, waits for them, and re-layouts  42.5 us (22%)
  matrix products  23.6 us (12%)
  starting transfers between devices  15.5 us (8%)
  between operations  14.1 us (7%)
  other arithmetic  13.5 us (7%)
    ppermute x8, waiting for transfers between devices, from_behind(): lax.ppermute(value, axis, [(source, source + steps) for source in range(l...  49 us
    all_gather x1, waiting for transfers between devices, shards(): lax.all_gather(gated, 'tp', axis=1, tiled=True)  33.9 us
    ppermute x8, starting transfers between devices, from_behind(): lax.ppermute(value, axis, [(source, source + steps) for source in range(l...  15.5 us
    unnamed x66, local copies, waits for them, and re-layouts  14.1 us
    another operation x2, local copies, waits for them, and re-layouts, toeplitz_taps(): tiled = jnp.tile(padded_taps, (1, FLEN))[:, :FLEN * 2 * FLEN]  9.73 us
    dot_general x8, matrix products, attend(): jnp.einsum('thd,shd->hts', query_heads, key_heads, preferred_element_type...  9.04 us
    reduce_sum x8, other arithmetic, attend(): row_sum = row_sum * rescale + jnp.sum(weights, axis=2)  5.82 us
    another operation x7, local copies, waits for them, and re-layouts, attend(): value_heads = key_value[1].reshape(span_rows, head_count, HEAD)  5.56 us
  transfers between devices with their start and end apart: 9, of which 8 were waited for; matrix products, arithmetic and copies ran while one was open for 22% of the time, Pallas kernels for 0%

commit v1 on v0

--- a/solution.py
+++ b/solution.py
@@ -82,7 +82,9 @@
     gated = (streams[0] * conv).astype(jnp.bfloat16)
     weights_local = proj_qk.reshape(proj_qk.shape[0], 2 * chan_width)
     projected = jnp.dot(
-        lax.all_gather(gated, "tp", axis=1, tiled=True),
+        jnp.concatenate(
+            lax.all_to_all(jnp.stack([gated] * lax.axis_size("tp")), "tp", 0, 0), axis=1
+        ),
         weights_local,
         preferred_element_type=jnp.float32,
     )

time: 193 us -> 154 us (0.80)
  waiting for transfers between devices: 82.9 us -> 50.9 us
  between operations: 14.1 us -> 0.54 us
  starting transfers between devices: 15.5 us -> 21.5 us
  other arithmetic: 13.5 us -> 10 us
  matrix products: 23.6 us -> 26.4 us
    all_gather x1 -> x0, waiting for transfers between devices: 33.9 us -> none  [shards(): lax.all_gather(gated, 'tp', axis=1, tiled=True)]
    all_to_all x0 -> x1, waiting for transfers between devices: none -> 6.76 us  [shards(): lax.all_to_all(jnp.stack([gated] * lax.axis_size('tp')), 'tp', 0, 0)]
    all_to_all x0 -> x1, starting transfers between devices: none -> 5.4 us  [shards(): lax.all_to_all(jnp.stack([gated] * lax.axis_size('tp')), 'tp', 0, 0)]
    ppermute x8, waiting for transfers between devices: 49 us -> 44.1 us  [from_behind(): lax.ppermute(value, axis, [(source, source + steps) for source in range(l...]
    dot_general x8, matrix products: 9.04 us -> 12.1 us  [attend(): jnp.einsum('thd,shd->hts', query_heads, key_heads, preferred_element_type...]
    add x4, other arithmetic: 2.26 us -> 0.03 us  [attend(): key_pos = key_offset + jnp.arange(span_rows, dtype=jnp.int32)]
    unnamed x66 -> x36, local copies, waits for them, and re-layouts: 14.1 us -> 14 us
  transfers between devices with their start and end apart: 9 -> 9, of which waited for: 8 -> 8; matrix products, arithmetic and copies ran while one was open for 22% -> 29% of each run, Pallas kernels for 0% -> 0%
where the time goes in v1:
time: 154 us; the launch traced here: 153 us
  waiting for transfers between devices  50.9 us (33%)
  local copies, waits for them, and re-layouts  43.2 us (28%)
  matrix products  26.4 us (17%)
  starting transfers between devices  21.5 us (14%)
  other arithmetic  10 us (6%)
    ppermute x8, waiting for transfers between devices, from_behind(): lax.ppermute(value, axis, [(source, source + steps) for source in range(l...  44.1 us
    ppermute x8, starting transfers between devices, from_behind(): lax.ppermute(value, axis, [(source, source + steps) for source in range(l...  16.1 us
    unnamed x36, local copies, waits for them, and re-layouts  14 us
    dot_general x8, matrix products, attend(): jnp.einsum('thd,shd->hts', query_heads, key_heads, preferred_element_type...  12.1 us
    another operation x2, local copies, waits for them, and re-layouts, toeplitz_taps(): tiled = jnp.tile(padded_taps, (1, FLEN))[:, :FLEN * 2 * FLEN]  9.7 us
    all_to_all x1, waiting for transfers between devices, shards(): lax.all_to_all(jnp.stack([gated] * lax.axis_size('tp')), 'tp', 0, 0)  6.76 us
    reduce_sum x8, other arithmetic, attend(): row_sum = row_sum * rescale + jnp.sum(weights, axis=2)  5.82 us
    another operation x7, local copies, waits for them, and re-layouts, attend(): value_heads = key_value[1].reshape(span_rows, head_count, HEAD)  5.54 us
  transfers between devices with their start and end apart: 9, of which 8 were waited for; matrix products, arithmetic and copies ran while one was open for 29% of the time, Pallas kernels for 0%

profile of v1, /device:TPU:128, one launch (start us, length us, event | category | flops | bytes accessed | tf_op | source)
XLA Modules:
  0.0 152.5 jit_solution(2984926848999120650)
XLA Ops:
  0.0 1.4 copy-done
  1.4 1.1 convolution_bitcast_fusion
  2.6 1.9 %collective-permute-start = (bf16[127,512]{1,0:T(8,128)(2,1)S(1)}, bf16[127,512]{1,0:T(8,128)(2,1)S(1)}, u32[]{:S(2)}, u32[]{:S(2)}) collective-permute-start(bf16[127,512]{1,0:T(8,128)(2,1)S(1)} %slice_bitcast_fusion.3), channel_id=1, source_target_pairs={{0,8},{8,16},{16,24},{24,32},{32,40},{40,48},{48,56},{56,64},{64,7... | collective-permute-start | bytes 390152 | tf_op jit(solution)/shard_map/ppermute | solution.py:15
  4.5 0.8 rev.3
  5.4 3.1 %tile.4 = f32[32,128,257]{2,1,0:T(8,128)} broadcast(f32[32,257]{1,0:T(8,128)S(1)} %maximum_maximum_fusion), dimensions={0,2} | broadcast | bytes 4243584 | tf_op jit(solution)/shard_map/tile | solution.py:57
  8.5 6.6 %tile.10 = f32[32,32896]{1,0:T(8,128)} reshape(f32[32,128,257]{2,1,0:T(8,128)} %tile.4) | data formatting | bytes 8421376 | tf_op jit(solution)/shard_map/tile | solution.py:57
  15.1 2.2 %slice-done = f32[32,32768]{1,0:T(8,128)S(1)} async-done(((f32[32,32896]{1,0:T(8,128)}), f32[32,32768]{1,0:T(8,128)S(1)}, s32[]{:S(2)}) %slice-start) | async-done | bytes 4194328 | tf_op jit(solution)/shard_map/slice | solution.py:57
  17.3 3.2 %copy.94 = f32[4,8,128,256]{3,2,1,0:T(8,128)} copy(f32[4,8,128,256]{3,1,2,0:T(8,128)S(1)} %bitcast.262) | data formatting | bytes 8388608
  21.0 5.3 %fusion.141 = f32[32,16,128]{2,1,0:T(8,128)S(1)} fusion(f32[256,32,16]{0,2,1:T(8,128)S(1)} %bitcast.268, f32[32,128,256]{2,1,0:T(8,128)} %bitcast.263), kind=kOutput, calls=%fused_computation.217 | convolution fusion | flops 201326592 | bytes 4980736 | tf_op jit(solution)/shard_map/gos,nsgc->nogc/dot_general | solution.py:79
  26.6 1.2 stack.9
  27.8 5.4 %all-to-all-start = ((bf16[8,128,512]{1,2,0:T(8,128)(2,1)}), bf16[8,128,512]{1,2,0:T(8,128)(2,1)S(1)}, u32[]{:S(2)}, u32[]{:S(2)}) async-start(bf16[8,128,512]{1,2,0:T(8,128)(2,1)} %stack.9), calls=%async_computation | async-start | bytes 2097152 | tf_op jit(solution)/shard_map/all_to_all | solution.py:86
  33.2 9.3 %copy.95 = bf16[512,8,2,512]{3,1,2,0:T(8,128)(2,1)} copy(bf16[512,8,2,512]{3,2,1,0:T(2,128)(2,1)} %bitcast.264) | data formatting | bytes 16777216
  42.7 6.8 %all-to-all-done = bf16[8,128,512]{1,2,0:T(8,128)(2,1)S(1)} async-done(((bf16[8,128,512]{1,2,0:T(8,128)(2,1)}), bf16[8,128,512]{1,2,0:T(8,128)(2,1)S(1)}, u32[]{:S(2)}, u32[]{:S(2)}) %all-to-all-start) | async-done | bytes 1048608 | tf_op jit(solution)/shard_map/all_to_all | solution.py:86
  49.4 4.7 %convolution_convert_fusion = bf16[128,1024]{1,0:T(8,128)(2,1)S(1)} fusion(bf16[128,4096]{0,1:T(8,128)(2,1)S(1)} %bitcast.265, bf16[4096,1024]{1,0:T(8,128)(2,1)} %bitcast.261), kind=kOutput, calls=%fused_computation.1 | convolution fusion | flops 1073872896 | bytes 9699328 | tf_op jit(solution)/shard_map/dot_general | solution.py:84
  54.2 2.7 %collective-permute-start.1 = (bf16[2,128,512]{2,1,0:T(8,128)(2,1)S(1)}, bf16[2,128,512]{2,1,0:T(8,128)(2,1)S(1)}, u32[]{:S(2)}, u32[]{:S(2)}) collective-permute-start(bf16[2,128,512]{2,1,0:T(8,128)(2,1)S(1)} %pad_maximum_fusion.1), channel_id=1, source_target_pairs={{0,8},{8,16},{16,24},{24,32},{32,40},{40,48},{48,56},{56,64},{64,7... | collective-permute-start | bytes 786440 | tf_op jit(solution)/shard_map/ppermute | solution.py:15
  56.9 1.0 compare_and_fusion.5
  57.9 0.8 copy.84
  58.7 1.5 fusion.140
  60.2 5.3 %collective-permute-done.1 = bf16[2,128,512]{2,1,0:T(8,128)(2,1)S(1)} collective-permute-done((bf16[2,128,512]{2,1,0:T(8,128)(2,1)S(1)}, bf16[2,128,512]{2,1,0:T(8,128)(2,1)S(1)}, u32[]{:S(2)}, u32[]{:S(2)}) %collective-permute-start.1) | collective-permute-done | bytes 262176 | tf_op jit(solution)/shard_map/ppermute | solution.py:15
  65.5 1.9 %collective-permute-start.2 = (bf16[2,128,512]{2,1,0:T(8,128)(2,1)S(1)}, bf16[2,128,512]{2,1,0:T(8,128)(2,1)S(1)}, u32[]{:S(2)}, u32[]{:S(2)}) collective-permute-start(bf16[2,128,512]{2,1,0:T(8,128)(2,1)S(1)} %collective-permute-done.1), channel_id=1, source_target_pairs={{0,8},{8,16},{16,24},{24,32},{32,40},{40,48},{48,56},{56,64},{64,7... | collective-permute-start | bytes 786440 | tf_op jit(solution)/shard_map/ppermute | solution.py:15
  67.6 0.8 fusion.139
  68.4 8.4 %collective-permute-done.2 = bf16[2,128,512]{2,1,0:T(8,128)(2,1)S(1)} collective-permute-done((bf16[2,128,512]{2,1,0:T(8,128)(2,1)S(1)}, bf16[2,128,512]{2,1,0:T(8,128)(2,1)S(1)}, u32[]{:S(2)}, u32[]{:S(2)}) %collective-permute-start.2) | collective-permute-done | bytes 262176 | tf_op jit(solution)/shard_map/ppermute | solution.py:15
  76.8 1.9 %collective-permute-start.3 = (bf16[2,128,512]{2,1,0:T(8,128)(2,1)S(1)}, bf16[2,128,512]{2,1,0:T(8,128)(2,1)S(1)}, u32[]{:S(2)}, u32[]{:S(2)}) collective-permute-start(bf16[2,128,512]{2,1,0:T(8,128)(2,1)S(1)} %collective-permute-done.2), channel_id=1, source_target_pairs={{0,8},{8,16},{16,24},{24,32},{32,40},{40,48},{48,56},{56,64},{64,7... | collective-permute-start | bytes 786440 | tf_op jit(solution)/shard_map/ppermute | solution.py:15
  80.1 1.7 %fusion.138 = (f32[4,128]{1,0:T(4,128)}, f32[4,128,128]{1,2,0:T(8,128)S(1)}) fusion(bf16[128,4,128]{2,1,0:T(4,128)(2,1)} %reshape_squeeze.44, bf16[16,4,8,128]{3,2,1,0:T(8,128)(2,1)S(1)} %get-tuple-element.41, pred[128,128]{0,1:T(8,128)(4,1)S(1)} %get-tuple-element.45), kind=kOutput, calls=%fused_computation.214 | convolution fusion | flops 16973312 | bytes 542720 | tf_op jit(solution)/shard_map/thd,shd->hts/dot_general | solution.py:26
  81.9 6.2 %collective-permute-done.3 = bf16[2,128,512]{2,1,0:T(8,128)(2,1)S(1)} collective-permute-done((bf16[2,128,512]{2,1,0:T(8,128)(2,1)S(1)}, bf16[2,128,512]{2,1,0:T(8,128)(2,1)S(1)}, u32[]{:S(2)}, u32[]{:S(2)}) %collective-permute-start.3) | collective-permute-done | bytes 262176 | tf_op jit(solution)/shard_map/ppermute | solution.py:15
  88.1 1.9 %collective-permute-start.4 = (bf16[2,128,512]{2,1,0:T(8,128)(2,1)S(1)}, bf16[2,128,512]{2,1,0:T(8,128)(2,1)S(1)}, u32[]{:S(2)}, u32[]{:S(2)}) collective-permute-start(bf16[2,128,512]{2,1,0:T(8,128)(2,1)S(1)} %collective-permute-done.3), channel_id=1, source_target_pairs={{0,8},{8,16},{16,24},{24,32},{32,40},{40,48},{48,56},{56,64},{64,7... | collective-permute-start | bytes 786440 | tf_op jit(solution)/shard_map/ppermute | solution.py:15
  90.8 1.7 %fusion.137 = (f32[4,128]{1,0:T(4,128)}, f32[4,128,128]{1,2,0:T(8,128)S(1)}) fusion(bf16[128,4,128]{2,1,0:T(4,128)(2,1)S(1)} %reshape_squeeze.46, bf16[16,4,8,128]{3,2,1,0:T(8,128)(2,1)} %copy-done.13, pred[128,128]{0,1:T(8,128)(4,1)} %get-tuple-element.46), kind=kOutput, calls=%fused_computation.213 | convolution fusion | flops 16973312 | bytes 542720 | tf_op jit(solution)/shard_map/thd,shd->hts/dot_general | solution.py:26
  92.5 6.8 %collective-permute-done.4 = bf16[2,128,512]{2,1,0:T(8,128)(2,1)S(1)} collective-permute-done((bf16[2,128,512]{2,1,0:T(8,128)(2,1)S(1)}, bf16[2,128,512]{2,1,0:T(8,128)(2,1)S(1)}, u32[]{:S(2)}, u32[]{:S(2)}) %collective-permute-start.4) | collective-permute-done | bytes 262176 | tf_op jit(solution)/shard_map/ppermute | solution.py:15
  100.1 1.9 %collective-permute-start.5 = (bf16[2,128,512]{2,1,0:T(8,128)(2,1)S(1)}, bf16[2,128,512]{2,1,0:T(8,128)(2,1)}, u32[]{:S(2)}, u32[]{:S(2)}) collective-permute-start(bf16[2,128,512]{2,1,0:T(8,128)(2,1)S(1)} %collective-permute-done.4), channel_id=1, source_target_pairs={{0,8},{8,16},{16,24},{24,32},{32,40},{40,48},{48,56},{56,64},{64,7... | collective-permute-start | bytes 786440 | tf_op jit(solution)/shard_map/ppermute | solution.py:15
  102.0 1.8 %fusion.136 = (f32[4,128]{1,0:T(4,128)}, f32[4,128,128]{1,2,0:T(8,128)S(1)}) fusion(bf16[128,4,128]{2,1,0:T(4,128)(2,1)} %reshape_squeeze.48, bf16[16,4,8,128]{3,2,1,0:T(8,128)(2,1)} %copy-done.13, pred[128,128]{0,1:T(8,128)(4,1)} %get-tuple-element.47), kind=kOutput, calls=%fused_computation.212 | convolution fusion | flops 16973312 | bytes 542720 | tf_op jit(solution)/shard_map/thd,shd->hts/dot_general | solution.py:26
  104.6 1.3 bitcast_maximum_fusion.2
  105.8 5.6 %collective-permute-done.5 = bf16[2,128,512]{2,1,0:T(8,128)(2,1)} collective-permute-done((bf16[2,128,512]{2,1,0:T(8,128)(2,1)S(1)}, bf16[2,128,512]{2,1,0:T(8,128)(2,1)}, u32[]{:S(2)}, u32[]{:S(2)}) %collective-permute-start.5) | collective-permute-done | bytes 262176 | tf_op jit(solution)/shard_map/ppermute | solution.py:15
  111.5 1.9 %collective-permute-start.6 = (bf16[2,128,512]{2,1,0:T(8,128)(2,1)}, bf16[2,128,512]{2,1,0:T(8,128)(2,1)}, u32[]{:S(2)}, u32[]{:S(2)}) collective-permute-start(bf16[2,128,512]{2,1,0:T(8,128)(2,1)} %collective-permute-done.5), channel_id=1, source_target_pairs={{0,8},{8,16},{16,24},{24,32},{32,40},{40,48},{48,56},{56,64},{64,7... | collective-permute-start | bytes 786440 | tf_op jit(solution)/shard_map/ppermute | solution.py:15
  113.4 1.0 fusion.128
  115.2 1.5 fusion.135
  116.7 6.4 %collective-permute-done.6 = bf16[2,128,512]{2,1,0:T(8,128)(2,1)} collective-permute-done((bf16[2,128,512]{2,1,0:T(8,128)(2,1)}, bf16[2,128,512]{2,1,0:T(8,128)(2,1)}, u32[]{:S(2)}, u32[]{:S(2)}) %collective-permute-start.6) | collective-permute-done | bytes 262176 | tf_op jit(solution)/shard_map/ppermute | solution.py:15
  123.1 1.9 %collective-permute-start.7 = (bf16[2,128,512]{2,1,0:T(8,128)(2,1)}, bf16[2,128,512]{2,1,0:T(8,128)(2,1)}, u32[]{:S(2)}, u32[]{:S(2)}) collective-permute-start(bf16[2,128,512]{2,1,0:T(8,128)(2,1)} %collective-permute-done.6), channel_id=1, source_target_pairs={{0,8},{8,16},{16,24},{24,32},{32,40},{40,48},{48,56},{56,64},{64,7... | collective-permute-start | bytes 786440 | tf_op jit(solution)/shard_map/ppermute | solution.py:15
  125.0 1.0 fusion.127
  127.5 1.8 %fusion.134 = (f32[4,128]{1,0:T(4,128)}, f32[4,128,128]{1,2,0:T(8,128)S(1)}) fusion(bf16[128,4,128]{2,1,0:T(4,128)(2,1)} %reshape_squeeze.52, bf16[16,4,8,128]{3,2,1,0:T(8,128)(2,1)} %copy-done.13, pred[128,128]{0,1:T(8,128)(4,1)S(1)} %get-tuple-element.49), kind=kOutput, calls=%fused_computation.210 | convolution fusion | flops 16973312 | bytes 542720 | tf_op jit(solution)/shard_map/thd,shd->hts/dot_general | solution.py:26
  129.2 5.5 %collective-permute-done.7 = bf16[2,128,512]{2,1,0:T(8,128)(2,1)} collective-permute-done((bf16[2,128,512]{2,1,0:T(8,128)(2,1)}, bf16[2,128,512]{2,1,0:T(8,128)(2,1)}, u32[]{:S(2)}, u32[]{:S(2)}) %collective-permute-start.7) | collective-permute-done | bytes 262176 | tf_op jit(solution)/shard_map/ppermute | solution.py:15
  134.7 1.7 %fusion.126 = (bf16[1,128,512]{2,1,0:T(8,128)(2,1)}, bf16[1,128,512]{2,1,0:T(8,128)(2,1)}) fusion(bf16[2,128,512]{2,1,0:T(8,128)(2,1)} %collective-permute-done.7), kind=kLoop, calls=%fused_computation.202 | loop fusion | bytes 524288 | tf_op jit(solution)/shard_map/slice | solution.py:25
  136.4 1.6 %reshape_squeeze.54 = bf16[128,4,128]{2,1,0:T(4,128)(2,1)} reshape(bf16[1,128,512]{2,1,0:T(8,128)(2,1)} %get-tuple-element.26) | data formatting | bytes 262144 | tf_op jit(solution)/shard_map/reshape;squeeze | solution.py:24
  138.0 1.7 %copy.91 = bf16[1,128,512]{1,2,0:T(8,128)(2,1)} copy(bf16[1,128,512]{2,1,0:T(8,128)(2,1)} %get-tuple-element.25) | data formatting | bytes 262144 | tf_op jit(solution)/shard_map/reshape;squeeze | solution.py:25
  139.7 1.3 fusion.133
  142.6 0.8 fusion.38
  146.6 1.0 fusion.28
  148.3 1.2 fusion.23
  149.6 0.9 fusion.21
  (91 shorter events, 14.7 us)
Async XLA Ops:
  0.0 1.4 copy-start
  2.6 18.1 %collective-permute-start = (bf16[127,512]{1,0:T(8,128)(2,1)S(1)}, bf16[127,512]{1,0:T(8,128)(2,1)S(1)}, u32[]{:S(2)}, u32[]{:S(2)}) collective-permute-start(bf16[127,512]{1,0:T(8,128)(2,1)S(1)} %slice_bitcast_fusion.3), channel_id=1, source_target_pairs={{0,8},{8,16},{16,24},{24,32},{32,40},{40,48},{48,56},{56,64},{64,7... | collective-permute-start | bytes 390152 | tf_op jit(solution)/shard_map/ppermute | solution.py:15
  15.1 2.2 %slice-start = ((f32[32,32896]{1,0:T(8,128)}), f32[32,32768]{1,0:T(8,128)S(1)}, s32[]{:S(2)}) async-start(f32[32,32896]{1,0:T(8,128)} %tile.10), calls=%async_computation.1 | async-start | bytes 8388608 | tf_op jit(solution)/shard_map/slice | solution.py:57
  27.8 21.6 %all-to-all-start = ((bf16[8,128,512]{1,2,0:T(8,128)(2,1)}), bf16[8,128,512]{1,2,0:T(8,128)(2,1)S(1)}, u32[]{:S(2)}, u32[]{:S(2)}) async-start(bf16[8,128,512]{1,2,0:T(8,128)(2,1)} %stack.9), calls=%async_computation | async-start | bytes 2097152 | tf_op jit(solution)/shard_map/all_to_all | solution.py:86
  54.1 33.9 %copy-start.13 = (bf16[16,4,8,128]{3,2,1,0:T(8,128)(2,1)}, bf16[16,4,8,128]{3,2,1,0:T(8,128)(2,1)S(1)}, u32[]{:S(2)}) copy-start(bf16[16,4,8,128]{3,2,1,0:T(8,128)(2,1)S(1)} %get-tuple-element.41) | copy-start | bytes 393220
  54.2 11.3 %collective-permute-start.1 = (bf16[2,128,512]{2,1,0:T(8,128)(2,1)S(1)}, bf16[2,128,512]{2,1,0:T(8,128)(2,1)S(1)}, u32[]{:S(2)}, u32[]{:S(2)}) collective-permute-start(bf16[2,128,512]{2,1,0:T(8,128)(2,1)S(1)} %pad_maximum_fusion.1), channel_id=1, source_target_pairs={{0,8},{8,16},{16,24},{24,32},{32,40},{40,48},{48,56},{56,64},{64,7... | collective-permute-start | bytes 786440 | tf_op jit(solution)/shard_map/ppermute | solution.py:15
  57.8 7.6 %copy-start.12 = (pred[128,128]{0,1:T(8,128)(4,1)}, pred[128,128]{0,1:T(8,128)(4,1)S(1)}, u32[]{:S(2)}) copy-start(pred[128,128]{0,1:T(8,128)(4,1)S(1)} %get-tuple-element.51) | copy-start | bytes 49156
  57.8 30.2 %copy-start.9 = (pred[128,128]{0,1:T(8,128)(4,1)}, pred[128,128]{0,1:T(8,128)(4,1)S(1)}, u32[]{:S(2)}) copy-start(pred[128,128]{0,1:T(8,128)(4,1)S(1)} %get-tuple-element.45) | copy-start | bytes 49156
  57.9 30.2 %copy-start.11 = (pred[128,128]{0,1:T(8,128)(4,1)}, pred[128,128]{0,1:T(8,128)(4,1)S(1)}, u32[]{:S(2)}) copy-start(pred[128,128]{0,1:T(8,128)(4,1)S(1)} %get-tuple-element.52) | copy-start | bytes 49156
  65.5 11.3 %collective-permute-start.2 = (bf16[2,128,512]{2,1,0:T(8,128)(2,1)S(1)}, bf16[2,128,512]{2,1,0:T(8,128)(2,1)S(1)}, u32[]{:S(2)}, u32[]{:S(2)}) collective-permute-start(bf16[2,128,512]{2,1,0:T(8,128)(2,1)S(1)} %collective-permute-done.1), channel_id=1, source_target_pairs={{0,8},{8,16},{16,24},{24,32},{32,40},{40,48},{48,56},{56,64},{64,7... | collective-permute-start | bytes 786440 | tf_op jit(solution)/shard_map/ppermute | solution.py:15
  76.8 11.3 %collective-permute-start.3 = (bf16[2,128,512]{2,1,0:T(8,128)(2,1)S(1)}, bf16[2,128,512]{2,1,0:T(8,128)(2,1)S(1)}, u32[]{:S(2)}, u32[]{:S(2)}) collective-permute-start(bf16[2,128,512]{2,1,0:T(8,128)(2,1)S(1)} %collective-permute-done.2), channel_id=1, source_target_pairs={{0,8},{8,16},{16,24},{24,32},{32,40},{40,48},{48,56},{56,64},{64,7... | collective-permute-start | bytes 786440 | tf_op jit(solution)/shard_map/ppermute | solution.py:15
  88.1 11.3 %collective-permute-start.4 = (bf16[2,128,512]{2,1,0:T(8,128)(2,1)S(1)}, bf16[2,128,512]{2,1,0:T(8,128)(2,1)S(1)}, u32[]{:S(2)}, u32[]{:S(2)}) collective-permute-start(bf16[2,128,512]{2,1,0:T(8,128)(2,1)S(1)} %collective-permute-done.3), channel_id=1, source_target_pairs={{0,8},{8,16},{16,24},{24,32},{32,40},{40,48},{48,56},{56,64},{64,7... | collective-permute-start | bytes 786440 | tf_op jit(solution)/shard_map/ppermute | solution.py:15
  90.0 25.2 %copy-start.14 = (bf16[16,4,8,128]{3,2,1,0:T(8,128)(2,1)S(1)}, bf16[16,4,8,128]{3,2,1,0:T(8,128)(2,1)}, u32[]{:S(2)}) copy-start(bf16[16,4,8,128]{3,2,1,0:T(8,128)(2,1)} %copy-done.13) | copy-start | bytes 393220
  100.1 11.4 %collective-permute-start.5 = (bf16[2,128,512]{2,1,0:T(8,128)(2,1)S(1)}, bf16[2,128,512]{2,1,0:T(8,128)(2,1)}, u32[]{:S(2)}, u32[]{:S(2)}) collective-permute-start(bf16[2,128,512]{2,1,0:T(8,128)(2,1)S(1)} %collective-permute-done.4), channel_id=1, source_target_pairs={{0,8},{8,16},{16,24},{24,32},{32,40},{40,48},{48,56},{56,64},{64,7... | collective-permute-start | bytes 786440 | tf_op jit(solution)/shard_map/ppermute | solution.py:15
  111.5 11.6 %collective-permute-start.6 = (bf16[2,128,512]{2,1,0:T(8,128)(2,1)}, bf16[2,128,512]{2,1,0:T(8,128)(2,1)}, u32[]{:S(2)}, u32[]{:S(2)}) collective-permute-start(bf16[2,128,512]{2,1,0:T(8,128)(2,1)} %collective-permute-done.5), channel_id=1, source_target_pairs={{0,8},{8,16},{16,24},{24,32},{32,40},{40,48},{48,56},{56,64},{64,7... | collective-permute-start | bytes 786440 | tf_op jit(solution)/shard_map/ppermute | solution.py:15
  123.1 11.6 %collective-permute-start.7 = (bf16[2,128,512]{2,1,0:T(8,128)(2,1)}, bf16[2,128,512]{2,1,0:T(8,128)(2,1)}, u32[]{:S(2)}, u32[]{:S(2)}) collective-permute-start(bf16[2,128,512]{2,1,0:T(8,128)(2,1)} %collective-permute-done.6), channel_id=1, source_target_pairs={{0,8},{8,16},{16,24},{24,32},{32,40},{40,48},{48,56},{56,64},{64,7... | collective-permute-start | bytes 786440 | tf_op jit(solution)/shard_map/ppermute | solution.py:15
  139.6 10.8 %copy-start.1 = (bf16[1,128,512]{1,2,0:T(8,128)(2,1)S(1)}, bf16[1,128,512]{1,2,0:T(8,128)(2,1)}, u32[]{:S(2)}) copy-start(bf16[1,128,512]{1,2,0:T(8,128)(2,1)} %copy.86) | copy-start | bytes 393220
  139.6 10.8 %copy-start.10 = (pred[128,128]{0,1:T(8,128)(4,1)S(1)}, pred[128,128]{0,1:T(8,128)(4,1)}, u32[]{:S(2)}) copy-start(pred[128,128]{0,1:T(8,128)(4,1)} %copy-done.9) | copy-start | bytes 49156
  139.6 11.1 %copy-start.2 = (bf16[1,128,512]{1,2,0:T(8,128)(2,1)S(1)}, bf16[1,128,512]{1,2,0:T(8,128)(2,1)}, u32[]{:S(2)}) copy-start(bf16[1,128,512]{1,2,0:T(8,128)(2,1)} %copy.87) | copy-start | bytes 393220
  139.6 11.1 %copy-start.8 = (pred[128,128]{0,1:T(8,128)(4,1)S(1)}, pred[128,128]{0,1:T(8,128)(4,1)}, u32[]{:S(2)}) copy-start(pred[128,128]{0,1:T(8,128)(4,1)} %get-tuple-element.46) | copy-start | bytes 49156
  139.6 11.3 %copy-start.3 = (bf16[1,128,512]{1,2,0:T(8,128)(2,1)S(1)}, bf16[1,128,512]{1,2,0:T(8,128)(2,1)}, u32[]{:S(2)}) copy-start(bf16[1,128,512]{1,2,0:T(8,128)(2,1)} %copy.88) | copy-start | bytes 393220
  139.6 11.3 %copy-start.7 = (pred[128,128]{0,1:T(8,128)(4,1)S(1)}, pred[128,128]{0,1:T(8,128)(4,1)}, u32[]{:S(2)}) copy-start(pred[128,128]{0,1:T(8,128)(4,1)} %get-tuple-element.47) | copy-start | bytes 49156
  139.7 11.5 %copy-start.4 = (bf16[1,128,512]{1,2,0:T(8,128)(2,1)S(1)}, bf16[1,128,512]{1,2,0:T(8,128)(2,1)}, u32[]{:S(2)}) copy-start(bf16[1,128,512]{1,2,0:T(8,128)(2,1)} %copy.89) | copy-start | bytes 393220
  139.7 11.5 %copy-start.6 = (pred[128,128]{0,1:T(8,128)(4,1)S(1)}, pred[128,128]{0,1:T(8,128)(4,1)}, u32[]{:S(2)}) copy-start(pred[128,128]{0,1:T(8,128)(4,1)} %get-tuple-element.48) | copy-start | bytes 49156
  141.0 10.4 %copy-start.5 = (bf16[1,128,512]{1,2,0:T(8,128)(2,1)S(1)}, bf16[1,128,512]{1,2,0:T(8,128)(2,1)}, u32[]{:S(2)}) copy-start(bf16[1,128,512]{1,2,0:T(8,128)(2,1)} %copy.90) | copy-start | bytes 393220
  142.6 9.0 %copy-start.15 = (bf16[1,128,512]{1,2,0:T(8,128)(2,1)S(1)}, bf16[1,128,512]{1,2,0:T(8,128)(2,1)}, u32[]{:S(2)}) copy-start(bf16[1,128,512]{1,2,0:T(8,128)(2,1)} %copy.91) | copy-start | bytes 393220
  142.6 9.0 %copy-start.16 = (pred[128,128]{0,1:T(8,128)(4,1)S(1)}, pred[128,128]{0,1:T(8,128)(4,1)}, u32[]{:S(2)}) copy-start(pred[128,128]{0,1:T(8,128)(4,1)} %get-tuple-element.50) | copy-start | bytes 49156
